TPU v7x, 512 devices: a whole 4x8x8 slice. The times are simulated.
512 devices in a mesh: sector: 32 (over z_hi, x, core), dof: 16 (over z_lo, y).
Axes of the slice: x: 4, y: 8, z: 8 (z_hi: 4, z_lo: 2; z = z_hi * 2 + z_lo), core: 2. Of those that a mesh axis runs over, the one named last changes fastest.
Arguments:
- rhs: float32 [32, 4096, 128], P('sector', 'dof')
- diagonal: float32 [32, 4096], P('sector', 'dof'), may hold values from 4 to 8
- coupling: bfloat16 [32, 4096, 2048], P('sector', 'dof'), may hold values from -0.125 to 0.125
- springs: float32 [32, 3072], P('sector', 'dof'), may hold values from 1 to 4
- precond: bfloat16 [4096, 4096], P('dof')
- hub_inverse: bfloat16 [3072, 3072], P('dof')
Outputs:
- solution: float32 [32, 4096, 128], P('sector', 'dof')
- residual: float32 [32, 4096, 128], P('sector', 'dof')
All inputs are finite; a program needn't handle non-finite values.
Results may differ from a plain program's by a relative error of at most 0.0056.
Values may be sent and summed in bfloat16 or wider, within the bound.
A program may use at most 64 MiB of HBM per device.

v0:
```python
import jax
import jax.numpy as jnp
from jax import lax
from jax.sharding import PartitionSpec as P

ITERS = 3


def extended(cells, sides, width):
    for axis, dim in sides:
        count = lax.axis_size(axis)
        head = lax.slice_in_dim(cells, 0, width, axis=dim)
        tail = lax.slice_in_dim(cells, cells.shape[dim] - width, cells.shape[dim], axis=dim)
        cells = jnp.concatenate(
            [
                lax.ppermute(tail, axis, [(i, (i + 1) % count) for i in range(count)]),
                cells,
                lax.ppermute(head, axis, [((i + 1) % count, i) for i in range(count)]),
            ],
            axis=dim,
        )
    return cells


def fold_rows(field, update, start_value):
    return update(start_value, lax.all_gather(field, "dof", axis=0, tiled=True), jnp.int32(0))


def product_with(matrix):

    def update(total, piece, start):
        return jnp.dot(matrix, piece, preferred_element_type=jnp.float32)

    return update


def place_rows(total, piece, start):
    return piece


def body(rhs, diagonal, coupling, springs, precond, hub_inverse):
    residual = rhs[0]
    diag_rows = diagonal[0]
    couple_rows = coupling[0]
    spring_rows = springs[0][:, None]
    rows_dev = residual.shape[0]
    loads = residual.shape[1]
    quarter = rows_dev // 4
    parts = lax.axis_size("dof")
    solution = jnp.zeros_like(residual)
    for step in range(ITERS):
        precon = fold_rows(
            residual.astype(jnp.bfloat16),
            product_with(precond),
            jnp.zeros((rows_dev, loads), jnp.float32),
        )
        precon_low = precon.astype(jnp.bfloat16)
        own_faces = precon_low[: 2 * quarter]
        whole = fold_rows(
            own_faces, place_rows, jnp.zeros((parts * 2 * quarter, loads), jnp.bfloat16)
        )
        beside_all = extended(whole[None], (("sector", 0),), 1)
        prev_side = beside_all[0].reshape(parts, 2, quarter, loads)[:, 1]
        next_side = beside_all[2].reshape(parts, 2, quarter, loads)[:, 0]
        needed = jnp.stack([prev_side, next_side], axis=1).reshape(parts * 2 * quarter, loads)
        couple = jnp.dot(couple_rows, needed, preferred_element_type=jnp.float32)
        attached = precon[: 3 * quarter]
        load = lax.psum(spring_rows * attached, "sector")
        hub = fold_rows(
            load.astype(jnp.bfloat16),
            product_with(hub_inverse),
            jnp.zeros((3 * quarter, loads), jnp.float32),
        )
        hub_term = jnp.concatenate(
            [spring_rows * (attached - hub), jnp.zeros((quarter, loads), jnp.float32)], axis=0
        )
        image = diag_rows[:, None] * precon + couple + hub_term
        upper, lower = lax.psum(
            (jnp.sum(image * residual, axis=0), jnp.sum(image * image, axis=0)), ("sector", "dof")
        )
        alpha = upper / (lower + 1e-06)
        solution = solution + alpha * precon
        residual = residual - alpha * image
    return (solution[None], residual[None])


def solution(mesh):
    placed = (
        P("sector", "dof", None),
        P("sector", "dof"),
        P("sector", "dof", None),
        P("sector", "dof"),
        P("dof", None),
        P("dof", None),
    )
    return jax.shard_map(
        body,
        mesh=mesh,
        in_specs=placed,
        out_specs=(P("sector", "dof", None), P("sector", "dof", None)),
        check_vma=False,
    )
```

profile of v0, /device:TPU:1, one launch (start us, length us, event | category | flops | bytes accessed | tf_op | source)
XLA Modules:
  0.0 1211.0 jit_solution(1387459577958328483)
XLA Ops:
  7.2 1.7 bitcast_convert_fusion
  9.0 68.9 %all-gather.4.cloned.1.call-done = bf16[4096,128]{1,0:T(8,128)(2,1)} async-done(((bf16[256,128]{1,0:T(8,128)(2,1)}), bf16[4096,128]{1,0:T(8,128)(2,1)}) %all-gather.4.cloned.1.call-update) | async-done | bytes 1048592 | tf_op jit(solution)/shard_map/all_gather | solution.py:26
  77.9 1.9 fusion.18
  79.8 30.4 %all_gather.28 = bf16[2048,128]{1,0:T(8,128)(2,1)} all-gather(bf16[128,128]{1,0:T(8,128)(2,1)S(1)} %slice.71), channel_id=1, replica_groups=mesh['sector'=32,'dof'=16] {'dof'}, dimensions={0}, use_global_device_ids=true | all-gather | bytes 557056 | tf_op jit(solution)/shard_map/all_gather | solution.py:26
  110.2 19.7 %collective-permute-start.1 = (bf16[1,2048,128]{2,1,0:T(8,128)(2,1)}, bf16[1,2048,128]{2,1,0:T(8,128)(2,1)}, u32[]{:S(2)}, u32[]{:S(2)}) collective-permute-start(bf16[1,2048,128]{2,1,0:T(8,128)(2,1)} %bitcast.2), channel_id=1, source_target_pairs={{16,0},{32,16},{48,32},{64,48},{80,64},{96,80},{112,96},{128,112},... | collective-permute-start | bytes 1572872 | tf_op jit(solution)/shard_map/ppermute | solution.py:18
  129.9 3.0 collective-permute-start
  132.9 0.1 slice_multiply_fusion.2
  133.0 139.5 %psum.63 = bf16[192,128]{1,0:T(8,128)(2,1)} all-reduce(f32[192,128]{1,0:T(8,128)S(1)} %slice_multiply_fusion.2), channel_id=1, replica_groups=mesh['sector'=32,'dof'=16] {'sector'}, use_global_device_ids=true, to_apply=%region_0.0 | all-reduce | flops 24576 | bytes 147456 | tf_op jit(solution)/shard_map/psum | solution.py:68
  272.6 28.3 %all_gather.29 = bf16[3072,128]{1,0:T(8,128)(2,1)S(1)} all-gather(bf16[192,128]{1,0:T(8,128)(2,1)} %psum.63), channel_id=1, replica_groups=mesh['sector'=32,'dof'=16] {'dof'}, dimensions={0}, use_global_device_ids=true | all-gather | bytes 835584 | tf_op jit(solution)/shard_map/all_gather | solution.py:26
  300.9 0.5 fusion.11
  301.4 1.0 slice.50
  302.3 1.0 slice.49
  303.3 0.1 pad_maximum_fusion
  303.4 1.1 multiply_reduce_fusion.4
  304.5 108.3 %all-reduce.5 = (f32[128]{0:T(128)}, f32[128]{0:T(128)}) all-reduce(f32[128]{0:T(128)S(1)} %get-tuple-element.7, f32[128]{0:T(128)S(1)} %get-tuple-element.6), channel_id=1, replica_groups=mesh['sector'=32,'dof'=16] {'sector','dof'}, use_global_device_ids=true, to_apply=%region_2.0 | all-reduce | flops 256 | bytes 2048 | tf_op jit(solution)/shard_map/psum | solution.py:78
  412.8 0.7 add_divide_fusion.2
  413.5 1.6 fusion.17
  415.2 56.7 %all-gather.6.cloned.1.call-done = bf16[4096,128]{1,0:T(8,128)(2,1)} async-done(((bf16[256,128]{1,0:T(8,128)(2,1)}), bf16[4096,128]{1,0:T(8,128)(2,1)}) %all-gather.6.cloned.1.call-update) | async-done | bytes 1048592 | tf_op jit(solution)/shard_map/all_gather | solution.py:26
  471.8 1.9 convolution_bitcast_fusion.1
  473.8 0.7 slice_multiply_fusion.1
  474.5 30.4 %all_gather.31 = bf16[2048,128]{1,0:T(8,128)(2,1)} all-gather(bf16[128,128]{1,0:T(8,128)(2,1)S(1)} %slice.70), channel_id=1, replica_groups=mesh['sector'=32,'dof'=16] {'dof'}, dimensions={0}, use_global_device_ids=true | all-gather | bytes 557056 | tf_op jit(solution)/shard_map/all_gather | solution.py:26
  504.9 19.7 %collective-permute-start.3 = (bf16[1,2048,128]{2,1,0:T(8,128)(2,1)}, bf16[1,2048,128]{2,1,0:T(8,128)(2,1)}, u32[]{:S(2)}, u32[]{:S(2)}) collective-permute-start(bf16[1,2048,128]{2,1,0:T(8,128)(2,1)} %bitcast.11), channel_id=1, source_target_pairs={{16,0},{32,16},{48,32},{64,48},{80,64},{96,80},{112,96},{128,112},... | collective-permute-start | bytes 1572872 | tf_op jit(solution)/shard_map/ppermute | solution.py:18
  524.6 3.0 collective-permute-start.2
  527.6 139.7 %psum.66 = bf16[192,128]{1,0:T(8,128)(2,1)} all-reduce(f32[192,128]{1,0:T(8,128)} %slice_multiply_fusion.1), channel_id=1, replica_groups=mesh['sector'=32,'dof'=16] {'sector'}, use_global_device_ids=true, to_apply=%region_5.0 | all-reduce | flops 24576 | bytes 147456 | tf_op jit(solution)/shard_map/psum | solution.py:68
  667.2 28.3 %all_gather.32 = bf16[3072,128]{1,0:T(8,128)(2,1)S(1)} all-gather(bf16[192,128]{1,0:T(8,128)(2,1)} %psum.66), channel_id=1, replica_groups=mesh['sector'=32,'dof'=16] {'dof'}, dimensions={0}, use_global_device_ids=true | all-gather | bytes 835584 | tf_op jit(solution)/shard_map/all_gather | solution.py:26
  695.5 0.5 fusion.9
  696.0 1.0 slice.54
  697.0 1.0 slice.53
  698.0 1.7 multiply_reduce_fusion.2
  699.7 108.3 %all-reduce.4 = (f32[128]{0:T(128)}, f32[128]{0:T(128)}) all-reduce(f32[128]{0:T(128)} %get-tuple-element.5, f32[128]{0:T(128)S(1)} %get-tuple-element.4), channel_id=1, replica_groups=mesh['sector'=32,'dof'=16] {'sector','dof'}, use_global_device_ids=true, to_apply=%region_7.0 | all-reduce | flops 256 | bytes 2048 | tf_op jit(solution)/shard_map/psum | solution.py:78
  808.1 0.6 add_divide_fusion.1
  808.7 1.7 fusion.16
  810.4 56.7 %all-gather.8.cloned.1.call-done = bf16[4096,128]{1,0:T(8,128)(2,1)} async-done(((bf16[256,128]{1,0:T(8,128)(2,1)}), bf16[4096,128]{1,0:T(8,128)(2,1)}) %all-gather.8.cloned.1.call-update) | async-done | bytes 1048592 | tf_op jit(solution)/shard_map/all_gather | solution.py:26
  867.0 1.9 convolution_bitcast_fusion
  869.0 0.6 copy-done.5
  869.6 0.7 slice_multiply_fusion
  870.4 30.4 %all_gather.34 = bf16[2048,128]{1,0:T(8,128)(2,1)} all-gather(bf16[128,128]{1,0:T(8,128)(2,1)S(1)} %slice.69), channel_id=1, replica_groups=mesh['sector'=32,'dof'=16] {'dof'}, dimensions={0}, use_global_device_ids=true | all-gather | bytes 557056 | tf_op jit(solution)/shard_map/all_gather | solution.py:26
  900.7 19.7 %collective-permute-start.5 = (bf16[1,2048,128]{2,1,0:T(8,128)(2,1)}, bf16[1,2048,128]{2,1,0:T(8,128)(2,1)}, u32[]{:S(2)}, u32[]{:S(2)}) collective-permute-start(bf16[1,2048,128]{2,1,0:T(8,128)(2,1)} %bitcast.18), channel_id=1, source_target_pairs={{16,0},{32,16},{48,32},{64,48},{80,64},{96,80},{112,96},{128,112},... | collective-permute-start | bytes 1572872 | tf_op jit(solution)/shard_map/ppermute | solution.py:18
  920.4 3.0 collective-permute-start.4
  923.4 139.7 %psum.69 = bf16[192,128]{1,0:T(8,128)(2,1)} all-reduce(f32[192,128]{1,0:T(8,128)} %slice_multiply_fusion), channel_id=1, replica_groups=mesh['sector'=32,'dof'=16] {'sector'}, use_global_device_ids=true, to_apply=%region_10.0 | all-reduce | flops 24576 | bytes 147456 | tf_op jit(solution)/shard_map/psum | solution.py:68
  1063.1 28.3 %all_gather.35 = bf16[3072,128]{1,0:T(8,128)(2,1)S(1)} all-gather(bf16[192,128]{1,0:T(8,128)(2,1)} %psum.69), channel_id=1, replica_groups=mesh['sector'=32,'dof'=16] {'dof'}, dimensions={0}, use_global_device_ids=true | all-gather | bytes 835584 | tf_op jit(solution)/shard_map/all_gather | solution.py:26
  1091.4 1.5 fusion.7
  1092.9 1.0 slice.58
  1093.9 1.0 slice.57
  1094.9 0.1 pad_maximum_fusion.2
  1095.0 0.5 multiply_reduce_fusion
  1095.4 108.3 %all-reduce.3 = (f32[128]{0:T(128)S(1)}, f32[128]{0:T(128)S(1)}) all-reduce(f32[128]{0:T(128)S(1)} %get-tuple-element.3, f32[128]{0:T(128)S(1)} %get-tuple-element.2), channel_id=1, replica_groups=mesh['sector'=32,'dof'=16] {'sector','dof'}, use_global_device_ids=true, to_apply=%region_12.0 | all-reduce | flops 256 | bytes 2048 | tf_op jit(solution)/shard_map/psum | solution.py:78
  1203.8 0.7 subtract_bitcast_fusion
  (44 shorter events, 0.3 us)
Async XLA Ops:
  7.2 70.7 %copy-start = (bf16[256,4096]{1,0:T(8,128)(2,1)S(1)}, bf16[256,4096]{1,0:T(8,128)(2,1)}, u32[]{:S(2)}) copy-start(bf16[256,4096]{1,0:T(8,128)(2,1)} %param.10) | copy-start | bytes 6291460
  7.2 125.7 %copy-start.12 = (f32[1,192]{1,0:T(1,128)S(1)}, f32[1,192]{1,0:T(1,128)}, u32[]{:S(2)}) copy-start(f32[1,192]{1,0:T(1,128)} %param.9) | copy-start | bytes 2308
  7.2 70.7 %all-gather.4.cloned.1.call-start = ((), (), s32[]{:S(2)}) async-start(), calls=%async_computation | async-start | bytes 1114112 | tf_op jit(solution)/shard_map/all_gather | solution.py:26
  8.9 291.9 %copy-start.1 = (bf16[192,3072]{1,0:T(8,128)(2,1)S(1)}, bf16[192,3072]{1,0:T(8,128)(2,1)}, u32[]{:S(2)}) copy-start(bf16[192,3072]{1,0:T(8,128)(2,1)} %param.11) | copy-start | bytes 3538948
  9.0 462.9 %all-gather.6.cloned.1.call-start = ((), (), s32[]{:S(2)}) async-start(), calls=%async_computation.1 | async-start | bytes 1114112 | tf_op jit(solution)/shard_map/all_gather | solution.py:26
  110.2 191.1 %collective-permute-start.1 = (bf16[1,2048,128]{2,1,0:T(8,128)(2,1)}, bf16[1,2048,128]{2,1,0:T(8,128)(2,1)}, u32[]{:S(2)}, u32[]{:S(2)}) collective-permute-start(bf16[1,2048,128]{2,1,0:T(8,128)(2,1)} %bitcast.2), channel_id=1, source_target_pairs={{16,0},{32,16},{48,32},{64,48},{80,64},{96,80},{112,96},{128,112},... | collective-permute-start | bytes 1572872 | tf_op jit(solution)/shard_map/ppermute | solution.py:18
  129.9 172.4 %collective-permute-start = (bf16[1,2048,128]{2,1,0:T(8,128)(2,1)}, bf16[1,2048,128]{2,1,0:T(8,128)(2,1)}, u32[]{:S(2)}, u32[]{:S(2)}) collective-permute-start(bf16[1,2048,128]{2,1,0:T(8,128)(2,1)} %bitcast.2), channel_id=1, source_target_pairs={{0,16},{16,32},{32,48},{48,64},{64,80},{80,96},{96,112},{112,128},... | collective-permute-start | bytes 1572872 | tf_op jit(solution)/shard_map/ppermute | solution.py:16
  300.8 2.5 copy-start.2
  300.8 2.6 copy-start.8
  300.8 2.6 copy-start.13
  415.1 451.9 %all-gather.8.cloned.1.call-start = ((), (), s32[]{:S(2)}) async-start(), calls=%async_computation.2 | async-start | bytes 1114112 | tf_op jit(solution)/shard_map/all_gather | solution.py:26
  504.9 191.1 %collective-permute-start.3 = (bf16[1,2048,128]{2,1,0:T(8,128)(2,1)}, bf16[1,2048,128]{2,1,0:T(8,128)(2,1)}, u32[]{:S(2)}, u32[]{:S(2)}) collective-permute-start(bf16[1,2048,128]{2,1,0:T(8,128)(2,1)} %bitcast.11), channel_id=1, source_target_pairs={{16,0},{32,16},{48,32},{64,48},{80,64},{96,80},{112,96},{128,112},... | collective-permute-start | bytes 1572872 | tf_op jit(solution)/shard_map/ppermute | solution.py:18
  524.6 172.4 %collective-permute-start.2 = (bf16[1,2048,128]{2,1,0:T(8,128)(2,1)}, bf16[1,2048,128]{2,1,0:T(8,128)(2,1)}, u32[]{:S(2)}, u32[]{:S(2)}) collective-permute-start(bf16[1,2048,128]{2,1,0:T(8,128)(2,1)} %bitcast.11), channel_id=1, source_target_pairs={{0,16},{16,32},{32,48},{48,64},{64,80},{80,96},{96,112},{112,128},... | collective-permute-start | bytes 1572872 | tf_op jit(solution)/shard_map/ppermute | solution.py:16
  695.5 2.5 copy-start.3
  695.5 2.5 copy-start.11
  869.0 0.7 copy-start.5
  900.7 192.1 %collective-permute-start.5 = (bf16[1,2048,128]{2,1,0:T(8,128)(2,1)}, bf16[1,2048,128]{2,1,0:T(8,128)(2,1)}, u32[]{:S(2)}, u32[]{:S(2)}) collective-permute-start(bf16[1,2048,128]{2,1,0:T(8,128)(2,1)} %bitcast.18), channel_id=1, source_target_pairs={{16,0},{32,16},{48,32},{64,48},{80,64},{96,80},{112,96},{128,112},... | collective-permute-start | bytes 1572872 | tf_op jit(solution)/shard_map/ppermute | solution.py:18
  920.4 173.5 %collective-permute-start.4 = (bf16[1,2048,128]{2,1,0:T(8,128)(2,1)}, bf16[1,2048,128]{2,1,0:T(8,128)(2,1)}, u32[]{:S(2)}, u32[]{:S(2)}) collective-permute-start(bf16[1,2048,128]{2,1,0:T(8,128)(2,1)} %bitcast.18), channel_id=1, source_target_pairs={{0,16},{16,32},{32,48},{48,64},{64,80},{80,96},{96,112},{112,128},... | collective-permute-start | bytes 1572872 | tf_op jit(solution)/shard_map/ppermute | solution.py:16
  1091.4 3.6 copy-start.4
  1091.4 3.6 copy-start.6
  1091.4 3.6 copy-start.9
  1092.8 110.9 %copy-start.7 = (f32[256,128]{1,0:T(8,128)S(1)}, f32[256,128]{1,0:T(8,128)}, u32[]{:S(2)}) copy-start(f32[256,128]{1,0:T(8,128)} %copy-done.5) | copy-start | bytes 393220
  1092.9 110.9 %copy-start.10 = (f32[256,128]{1,0:T(8,128)S(1)}, f32[256,128]{1,0:T(8,128)}, u32[]{:S(2)}) copy-start(f32[256,128]{1,0:T(8,128)} %get-tuple-element.15) | copy-start | bytes 393220
Sparse Core Ops, SparseCore 0:
  10.7 67.1 all-gather.3
  415.3 56.5 all-gather.5
  810.5 56.5 all-gather.7
where the time goes:
time: 1210 us
  blocking collectives  920 us (76%)
  waiting for transfers between devices  182 us (15%)
  starting transfers between devices  68.2 us (6%)
  between operations  14.1 us (1%)
    psum x3, blocking collectives, body(): load = lax.psum(spring_rows * attached, 'sector')  419 us
    psum x3, blocking collectives, body(): lax.psum((jnp.sum(image * residual, axis=0), jnp.sum(image * image, axis=...  325 us
    all_gather x3, waiting for transfers between devices, fold_rows(): lax.all_gather(field, 'dof', axis=0, tiled=True)  182 us
    all_gather x6, blocking collectives, fold_rows(): lax.all_gather(field, 'dof', axis=0, tiled=True)  176 us
    ppermute x3, starting transfers between devices, extended(): lax.ppermute(head, axis, [((i + 1) % count, i) for i in range(count)])  59 us
  transfers between devices with their start and end apart: 9, of which 3 were waited for; matrix products, arithmetic and copies ran while one was open for 0% of the time, Pallas kernels for 0%

commit v1 on v0

--- a/solution.py
+++ b/solution.py
@@ -2,6 +2,7 @@
 import jax.numpy as jnp
 from jax import lax
 from jax.sharding import PartitionSpec as P
+from jax.lax import all_to_all, axis_size
 
 ITERS = 3
 
@@ -23,7 +24,13 @@
 
 
 def fold_rows(field, update, start_value):
-    return update(start_value, lax.all_gather(field, "dof", axis=0, tiled=True), jnp.int32(0))
+    return update(
+        start_value,
+        jnp.concatenate(
+            all_to_all(jnp.stack([field for _ in range(axis_size("dof"))], 0), "dof", 0, 0), 0
+        ),
+        jnp.int32(0),
+    )
 
 
 def product_with(matrix):

time: 1210 us -> 951 us (0.79)
  waiting for transfers between devices: 182 us -> 11.1 us
  blocking collectives: 920 us -> 830 us
  between operations: 14.1 us -> 1.02 us
    all_gather x3 -> x0, waiting for transfers between devices: 182 us -> none  [fold_rows(): lax.all_gather(field, 'dof', axis=0, tiled=True)]
    all_gather x6 -> x0, blocking collectives: 176 us -> none  [fold_rows(): lax.all_gather(field, 'dof', axis=0, tiled=True)]
    all_to_all x0 -> x3, blocking collectives: none -> 93.7 us  [fold_rows(): all_to_all(jnp.stack([field for _ in range(axis_size('dof'))], 0), 'dof',...]
    all_to_all x0 -> x6, starting transfers between devices: none -> 40.9 us  [fold_rows(): all_to_all(jnp.stack([field for _ in range(axis_size('dof'))], 0), 'dof',...]
    ppermute x3, starting transfers between devices: 59 us -> 26.4 us  [extended(): lax.ppermute(head, axis, [((i + 1) % count, i) for i in range(count)])]
  transfers between devices with their start and end apart: 9 -> 12, of which waited for: 3 -> 6; matrix products, arithmetic and copies ran while one was open for 0% -> 1% of each run, Pallas kernels for 0% -> 0%
where the time goes in v1:
time: 951 us; the launch traced here: 950 us
  blocking collectives  830 us (87%)
  starting transfers between devices  73.1 us (8%)
  local copies, waits for them, and re-layouts  15.4 us (2%)
  waiting for transfers between devices  11.1 us (1%)
  matrix products  10.3 us (1%)
    psum x3, blocking collectives, body(): load = lax.psum(spring_rows * attached, 'sector')  417 us
    psum x3, blocking collectives, body(): lax.psum((jnp.sum(image * residual, axis=0), jnp.sum(image * image, axis=...  320 us
    all_to_all x3, blocking collectives, fold_rows(): all_to_all(jnp.stack([field for _ in range(axis_size('dof'))], 0), 'dof',...  93.7 us
    all_to_all x6, starting transfers between devices, fold_rows(): all_to_all(jnp.stack([field for _ in range(axis_size('dof'))], 0), 'dof',...  40.9 us
    ppermute x3, starting transfers between devices, extended(): lax.ppermute(head, axis, [((i + 1) % count, i) for i in range(count)])  26.4 us
  transfers between devices with their start and end apart: 12, of which 6 were waited for; matrix products, arithmetic and copies ran while one was open for 1% of the time, Pallas kernels for 0%

profile of v1, /device:TPU:1, one launch (start us, length us, event | category | flops | bytes accessed | tf_op | source)
XLA Modules:
  0.0 949.7 jit_solution(3345229381181475859)
XLA Ops:
  0.6 1.1 convert_bitcast_fusion
  1.9 34.3 %all_to_all.45 = bf16[16,256,128]{2,1,0:T(8,128)(2,1)S(1)} all-to-all(bf16[16,256,128]{2,1,0:T(8,128)(2,1)S(1)} %stack.27), channel_id=1, replica_groups=mesh['sector'=32,'dof'=16] {'dof'}, dimensions={0} | all-to-all | bytes 2097152 | tf_op jit(solution)/shard_map/all_to_all | solution.py:30
  37.0 0.9 stack.28
  37.9 6.0 all-to-all-start.1
  44.0 142.7 %psum.63 = bf16[192,128]{1,0:T(8,128)(2,1)} all-reduce(f32[192,128]{1,0:T(8,128)S(1)} %slice_multiply_fusion.2), channel_id=1, replica_groups=mesh['sector'=32,'dof'=16] {'sector'}, use_global_device_ids=true, to_apply=%region_0.0 | all-reduce | flops 24576 | bytes 147456 | tf_op jit(solution)/shard_map/psum | solution.py:75
  186.7 1.8 stack.30
  188.5 7.7 all-to-all-start.2
  196.2 8.8 collective-permute-start.1
  205.0 1.9 collective-permute-start
  206.9 2.7 all-to-all-done.2
  209.6 1.7 fusion.11
  211.3 1.0 slice.50
  212.3 1.0 collective-permute-done
  213.4 1.0 slice.49
  214.4 1.1 multiply_reduce_fusion.4
  215.5 106.5 %all-reduce.5 = (f32[128]{0:T(128)}, f32[128]{0:T(128)}) all-reduce(f32[128]{0:T(128)S(1)} %get-tuple-element.7, f32[128]{0:T(128)S(1)} %get-tuple-element.6), channel_id=1, replica_groups=mesh['sector'=32,'dof'=16] {'sector','dof'}, use_global_device_ids=true, to_apply=%region_2.0 | all-reduce | flops 256 | bytes 2048 | tf_op jit(solution)/shard_map/psum | solution.py:85
  322.7 1.6 fusion.17
  324.5 29.5 %all_to_all.46 = bf16[16,256,128]{2,1,0:T(8,128)(2,1)S(1)} all-to-all(bf16[16,256,128]{2,1,0:T(8,128)(2,1)S(1)} %stack.31), channel_id=1, replica_groups=mesh['sector'=32,'dof'=16] {'dof'}, dimensions={0} | all-to-all | bytes 2097152 | tf_op jit(solution)/shard_map/all_to_all | solution.py:30
  354.7 0.9 stack.32
  355.5 6.4 all-to-all-start.4
  362.7 137.0 %psum.66 = bf16[192,128]{1,0:T(8,128)(2,1)} all-reduce(f32[192,128]{1,0:T(8,128)} %slice_multiply_fusion.1), channel_id=1, replica_groups=mesh['sector'=32,'dof'=16] {'sector'}, use_global_device_ids=true, to_apply=%region_5.0 | all-reduce | flops 24576 | bytes 147456 | tf_op jit(solution)/shard_map/psum | solution.py:75
  499.7 1.8 stack.34
  501.5 7.2 all-to-all-start.5
  508.7 8.8 collective-permute-start.3
  517.5 1.9 collective-permute-start.2
  519.4 2.7 all-to-all-done.5
  522.1 1.7 fusion.9
  523.8 1.0 slice.54
  524.8 1.1 collective-permute-done.2
  525.9 1.0 slice.53
  526.9 1.6 multiply_reduce_fusion.2
  528.5 106.5 %all-reduce.4 = (f32[128]{0:T(128)}, f32[128]{0:T(128)}) all-reduce(f32[128]{0:T(128)} %get-tuple-element.5, f32[128]{0:T(128)S(1)} %get-tuple-element.4), channel_id=1, replica_groups=mesh['sector'=32,'dof'=16] {'sector','dof'}, use_global_device_ids=true, to_apply=%region_7.0 | all-reduce | flops 256 | bytes 2048 | tf_op jit(solution)/shard_map/psum | solution.py:85
  635.7 1.6 fusion.16
  637.5 29.9 %all_to_all.47 = bf16[16,256,128]{2,1,0:T(8,128)(2,1)S(1)} all-to-all(bf16[16,256,128]{2,1,0:T(8,128)(2,1)S(1)} %stack.35), channel_id=1, replica_groups=mesh['sector'=32,'dof'=16] {'dof'}, dimensions={0} | all-to-all | bytes 2097152 | tf_op jit(solution)/shard_map/all_to_all | solution.py:30
  668.8 0.9 stack.36
  669.7 6.4 all-to-all-start.7
  676.2 1.6 slice_multiply_fusion
  677.8 136.8 %psum.69 = bf16[192,128]{1,0:T(8,128)(2,1)} all-reduce(f32[192,128]{1,0:T(8,128)} %slice_multiply_fusion), channel_id=1, replica_groups=mesh['sector'=32,'dof'=16] {'sector'}, use_global_device_ids=true, to_apply=%region_10.0 | all-reduce | flops 24576 | bytes 147456 | tf_op jit(solution)/shard_map/psum | solution.py:75
  814.6 1.8 stack.38
  816.5 7.3 all-to-all-start.8
  823.7 8.8 collective-permute-start.5
  832.5 1.9 collective-permute-start.4
  834.4 2.7 all-to-all-done.8
  837.1 1.7 fusion.7
  838.9 1.0 slice.58
  839.9 1.0 collective-permute-done.4
  840.9 1.0 slice.57
  842.4 106.5 %all-reduce.3 = (f32[128]{0:T(128)S(1)}, f32[128]{0:T(128)S(1)}) all-reduce(f32[128]{0:T(128)S(1)} %get-tuple-element.3, f32[128]{0:T(128)S(1)} %get-tuple-element.2), channel_id=1, replica_groups=mesh['sector'=32,'dof'=16] {'sector','dof'}, use_global_device_ids=true, to_apply=%region_12.0 | all-reduce | flops 256 | bytes 2048 | tf_op jit(solution)/shard_map/psum | solution.py:85
  (53 shorter events, 6.9 us)
Async XLA Ops:
  0.6 35.6 %copy-start = (bf16[256,4096]{1,0:T(8,128)(2,1)S(1)}, bf16[256,4096]{1,0:T(8,128)(2,1)}, u32[]{:S(2)}) copy-start(bf16[256,4096]{1,0:T(8,128)(2,1)} %param.10) | copy-start | bytes 6291460
  36.2 7.7 copy-start.12
  37.0 172.7 %copy-start.1 = (bf16[192,3072]{1,0:T(8,128)(2,1)S(1)}, bf16[192,3072]{1,0:T(8,128)(2,1)}, u32[]{:S(2)}) copy-start(bf16[192,3072]{1,0:T(8,128)(2,1)} %param.11) | copy-start | bytes 3538948
  37.9 148.8 %all-to-all-start.1 = ((bf16[16,128,128]{2,1,0:T(8,128)(2,1)}), bf16[16,128,128]{2,1,0:T(8,128)(2,1)}, u32[]{:S(2)}, u32[]{:S(2)}) async-start(bf16[16,128,128]{2,1,0:T(8,128)(2,1)} %stack.28), calls=%async_computation.1 | async-start | bytes 1048576 | tf_op jit(solution)/shard_map/all_to_all | solution.py:30
  188.5 21.1 %all-to-all-start.2 = ((bf16[16,192,128]{2,1,0:T(8,128)(2,1)}), bf16[16,192,128]{2,1,0:T(8,128)(2,1)}, u32[]{:S(2)}, u32[]{:S(2)}) async-start(bf16[16,192,128]{2,1,0:T(8,128)(2,1)} %stack.30), calls=%async_computation.2 | async-start | bytes 1572864 | tf_op jit(solution)/shard_map/all_to_all | solution.py:30
  196.2 15.1 %collective-permute-start.1 = (bf16[1,2048,128]{2,1,0:T(8,128)(2,1)}, bf16[1,2048,128]{2,1,0:T(8,128)(2,1)}, u32[]{:S(2)}, u32[]{:S(2)}) collective-permute-start(bf16[1,2048,128]{2,1,0:T(8,128)(2,1)} %bitcast.3), channel_id=1, source_target_pairs={{16,0},{32,16},{48,32},{64,48},{80,64},{96,80},{112,96},{128,112},... | collective-permute-start | bytes 1572872 | tf_op jit(solution)/shard_map/ppermute | solution.py:19
  205.0 8.3 collective-permute-start
  209.6 4.8 copy-start.2
  209.6 4.8 copy-start.8
  209.6 4.8 copy-start.13
  355.5 144.2 %all-to-all-start.4 = ((bf16[16,128,128]{2,1,0:T(8,128)(2,1)}), bf16[16,128,128]{2,1,0:T(8,128)(2,1)}, u32[]{:S(2)}, u32[]{:S(2)}) async-start(bf16[16,128,128]{2,1,0:T(8,128)(2,1)} %stack.32), calls=%async_computation.4 | async-start | bytes 1048576 | tf_op jit(solution)/shard_map/all_to_all | solution.py:30
  501.5 20.6 %all-to-all-start.5 = ((bf16[16,192,128]{2,1,0:T(8,128)(2,1)}), bf16[16,192,128]{2,1,0:T(8,128)(2,1)}, u32[]{:S(2)}, u32[]{:S(2)}) async-start(bf16[16,192,128]{2,1,0:T(8,128)(2,1)} %stack.34), calls=%async_computation.5 | async-start | bytes 1572864 | tf_op jit(solution)/shard_map/all_to_all | solution.py:30
  508.7 15.1 %collective-permute-start.3 = (bf16[1,2048,128]{2,1,0:T(8,128)(2,1)}, bf16[1,2048,128]{2,1,0:T(8,128)(2,1)}, u32[]{:S(2)}, u32[]{:S(2)}) collective-permute-start(bf16[1,2048,128]{2,1,0:T(8,128)(2,1)} %bitcast.15), channel_id=1, source_target_pairs={{16,0},{32,16},{48,32},{64,48},{80,64},{96,80},{112,96},{128,112},... | collective-permute-start | bytes 1572872 | tf_op jit(solution)/shard_map/ppermute | solution.py:19
  517.5 8.3 collective-permute-start.2
  522.1 4.8 copy-start.3
  522.1 4.8 copy-start.11
  668.1 0.7 copy-start.5
  669.7 144.9 %all-to-all-start.7 = ((bf16[16,128,128]{2,1,0:T(8,128)(2,1)}), bf16[16,128,128]{2,1,0:T(8,128)(2,1)}, u32[]{:S(2)}, u32[]{:S(2)}) async-start(bf16[16,128,128]{2,1,0:T(8,128)(2,1)} %stack.36), calls=%async_computation.7 | async-start | bytes 1048576 | tf_op jit(solution)/shard_map/all_to_all | solution.py:30
  816.5 20.7 %all-to-all-start.8 = ((bf16[16,192,128]{2,1,0:T(8,128)(2,1)}), bf16[16,192,128]{2,1,0:T(8,128)(2,1)}, u32[]{:S(2)}, u32[]{:S(2)}) async-start(bf16[16,192,128]{2,1,0:T(8,128)(2,1)} %stack.38), calls=%async_computation.8 | async-start | bytes 1572864 | tf_op jit(solution)/shard_map/all_to_all | solution.py:30
  823.7 15.1 %collective-permute-start.5 = (bf16[1,2048,128]{2,1,0:T(8,128)(2,1)}, bf16[1,2048,128]{2,1,0:T(8,128)(2,1)}, u32[]{:S(2)}, u32[]{:S(2)}) collective-permute-start(bf16[1,2048,128]{2,1,0:T(8,128)(2,1)} %bitcast.24), channel_id=1, source_target_pairs={{16,0},{32,16},{48,32},{64,48},{80,64},{96,80},{112,96},{128,112},... | collective-permute-start | bytes 1572872 | tf_op jit(solution)/shard_map/ppermute | solution.py:19
  832.5 8.3 collective-permute-start.4
  837.1 4.8 copy-start.4
  837.1 4.8 copy-start.6
  837.1 4.8 copy-start.9
  838.8 110.1 %copy-start.7 = (f32[256,128]{1,0:T(8,128)S(1)}, f32[256,128]{1,0:T(8,128)}, u32[]{:S(2)}) copy-start(f32[256,128]{1,0:T(8,128)} %copy-done.5) | copy-start | bytes 393220
  838.8 110.1 %copy-start.10 = (f32[256,128]{1,0:T(8,128)S(1)}, f32[256,128]{1,0:T(8,128)}, u32[]{:S(2)}) copy-start(f32[256,128]{1,0:T(8,128)} %get-tuple-element.15) | copy-start | bytes 393220
